TPU v7x, 32 devices: a whole 2x2x4 slice. The times are simulated.
32 devices in a mesh: attn: 4 (over y, core), expert: 4 (over z), loop: 2 (over x).
Axes of the slice: x: 2, y: 2, z: 4, core: 2. Of those that a mesh axis runs over, the one named last changes fastest.
Arguments:
- resid: bfloat16 [64, 3072], P(('expert', 'loop', 'attn')), may hold values from -33 to 33
- query: bfloat16 [64, 3072], P(('expert', 'loop', 'attn')), may hold values from -68.75573 to 68.75573
- key_cache: bfloat16 [64, 256, 512], P(('expert', 'loop', 'attn')), may hold values from -6 to 6
- value_cache: bfloat16 [64, 256, 512], P(('expert', 'loop', 'attn')), may hold values from -6 to 6
- new_key: bfloat16 [64, 512], P(('expert', 'loop', 'attn')), may hold values from -6 to 6
- new_value: bfloat16 [64, 512], P(('expert', 'loop', 'attn')), may hold values from -6 to 6
- cache_len: int32 [64], P(('expert', 'loop', 'attn')), may hold values from 2 to 256, as said below
- norm_gain: float32 [3072], replicated, may hold values from 0.5 to 1.5
- gate_weight: bfloat16 [4, 3072, 8192], P('expert', 'attn', 'loop'), may hold values from -0.109375 to 0.109375
- up_weight: bfloat16 [4, 3072, 8192], P('expert', 'attn', 'loop'), may hold values from -0.109375 to 0.109375
- down_weight: bfloat16 [4, 8192, 3072], P('expert', 'loop', 'attn'), may hold values from -0.0625 to 0.0625
- block_rows: int32 [4, 1, 128], P('expert'), may hold values from -1 to 63, as said below
- slot_weight: float32 [4, 1, 128], P('expert'), may hold values from 0.1 to 1
Outputs:
- layer_out: bfloat16 [64, 3072], P(('expert', 'loop', 'attn'))
Inputs may be any that keep to these rules, and one draw needn't show every extreme that they name: `block_rows`: each of the 64 rows is named in the lists of exactly two different experts and nowhere else; within a list the rows ascend and fill the slots from the first one on; unused slots hold -1. One expert, drawn from the seed, is named by exactly 32 rows; the other experts by nearly equal numbers of rows. `cache_len`: some row uses all 256 positions.
All inputs are finite; a program needn't handle non-finite values.
Results may differ from a plain program's by a relative error of at most 0.0054.
Values may be sent and summed in bfloat16 or wider, within the bound.
A program may use at most 128 MiB of HBM per device.

v0:
```python
import jax
import jax.numpy as jnp
from jax import lax
from jax.sharding import PartitionSpec as P

Q_HEADS = 24
KV_HEADS = 4
HEAD = 128
CACHE = 256


def attend(query, key_cache, value_cache, new_key, new_value, cache_len):
    rows_here = query.shape[0]
    groups = Q_HEADS // KV_HEADS
    score_scale = HEAD ** (-0.5)
    queries = query.reshape(rows_here, KV_HEADS, groups, HEAD)
    cached_keys = key_cache.reshape(rows_here, CACHE, KV_HEADS, HEAD)
    cached_values = value_cache.reshape(rows_here, CACHE, KV_HEADS, HEAD)
    own_keys = new_key.reshape(rows_here, KV_HEADS, HEAD)
    own_values = new_value.reshape(rows_here, KV_HEADS, 1, HEAD)
    scores = (
        jnp.einsum("rkgd,rlkd->rkgl", queries, cached_keys, preferred_element_type=jnp.float32)
        * score_scale
    )
    own_score = (
        jnp.einsum("rkgd,rkd->rkg", queries, own_keys, preferred_element_type=jnp.float32)
        * score_scale
    )
    cache_live = jnp.arange(CACHE)[None, :] < cache_len[:, None]
    scores = jnp.where(cache_live[:, None, None, :], scores, -jnp.inf)
    row_max = jnp.maximum(jnp.max(scores, axis=-1), own_score)
    cached_exp = jnp.exp(scores - row_max[..., None])
    own_exp = jnp.exp(own_score - row_max)
    denominator = jnp.sum(cached_exp, axis=-1) + own_exp
    cached_prob = (cached_exp / denominator[..., None]).astype(jnp.bfloat16)
    own_prob = (own_exp / denominator).astype(jnp.bfloat16)
    attended = jnp.einsum(
        "rkgl,rlkd->rkgd", cached_prob, cached_values, preferred_element_type=jnp.float32
    )
    attended = attended + jnp.einsum(
        "rkg,rkxd->rkgd", own_prob, own_values, preferred_element_type=jnp.float32
    )
    return attended.reshape(rows_here, Q_HEADS * HEAD)


def per_device(
    resid,
    query,
    key_cache,
    value_cache,
    new_key,
    new_value,
    cache_len,
    norm_gain,
    gate_weight,
    up_weight,
    down_weight,
    block_rows,
    slot_weight,
):
    attended = attend(query, key_cache, value_cache, new_key, new_value, cache_len)
    residual = (resid.astype(jnp.float32) + attended).astype(jnp.bfloat16)
    residual_wide = residual.astype(jnp.float32)
    normed = (
        residual_wide
        * lax.rsqrt(jnp.mean(residual_wide * residual_wide, axis=-1, keepdims=True) + 1e-05)
        * norm_gain
    ).astype(jnp.bfloat16)
    width_parts = lax.all_to_all(normed, "attn", split_axis=1, concat_axis=0, tiled=True)
    every_row = lax.all_gather(width_parts, ("expert", "loop"), axis=0, tiled=True)
    total_rows = every_row.shape[0]
    slot_total = block_rows.shape[1] * block_rows.shape[2]
    slot_rows = block_rows.reshape(slot_total)
    slot_live = slot_rows >= 0
    picked = jnp.take(every_row, jnp.where(slot_live, slot_rows, 0), axis=0)
    picked = jnp.where(slot_live[:, None], picked, jnp.zeros_like(picked))
    gate_part = jnp.dot(picked, gate_weight[0], preferred_element_type=jnp.float32)
    up_part = jnp.dot(picked, up_weight[0], preferred_element_type=jnp.float32)
    gate_total, up_total = lax.psum((gate_part, up_part), "attn")
    hidden = (jax.nn.silu(gate_total) * up_total).astype(jnp.bfloat16)
    expert_out = jnp.dot(hidden, down_weight[0], preferred_element_type=jnp.float32)
    weighted = expert_out * jnp.where(slot_live, slot_weight.reshape(slot_total), 0.0)[:, None]
    target = jnp.where(slot_live, slot_rows, total_rows)
    dense_rows = (
        jnp.zeros((total_rows, expert_out.shape[1]), jnp.float32)
        .at[target]
        .add(weighted, mode="drop")
    )
    owned_sums = lax.psum_scatter(
        dense_rows, ("expert", "loop"), scatter_dimension=0, tiled=True
    ).astype(jnp.bfloat16)
    returned = lax.all_to_all(owned_sums, "attn", split_axis=0, concat_axis=1, tiled=True)
    return (residual.astype(jnp.float32) + returned.astype(jnp.float32)).astype(jnp.bfloat16)


def solution(mesh):
    in_specs = (
        P(("expert", "loop", "attn"), None),
        P(("expert", "loop", "attn"), None),
        P(("expert", "loop", "attn"), None, None),
        P(("expert", "loop", "attn"), None, None),
        P(("expert", "loop", "attn"), None),
        P(("expert", "loop", "attn"), None),
        P(("expert", "loop", "attn")),
        P(),
        P("expert", "attn", "loop"),
        P("expert", "attn", "loop"),
        P("expert", "loop", "attn"),
        P("expert", None, None),
        P("expert", None, None),
    )
    out_specs = P(("expert", "loop", "attn"), None)
    return jax.shard_map(
        per_device, mesh=mesh, in_specs=in_specs, out_specs=out_specs, check_vma=False
    )
```

profile of v0, /device:TPU:0, one launch (start us, length us, event | category | flops | bytes accessed | tf_op | source)
XLA Modules:
  0.0 230.8 jit_solution(8481233316567846436)
XLA Ops:
  6.5 0.0 copy-start
  6.5 0.8 reshape.133
  7.3 0.7 iota_compare_fusion
  8.1 0.7 reshape.163
  8.7 0.1 fusion.30
  8.9 0.0 copy-done
  8.9 0.3 fusion.29
  9.2 0.2 fusion.17
  9.4 0.7 reshape.142
  10.1 1.3 convolution_add_fusion
  11.4 0.8 fusion.20
  12.3 1.4 fusion.22
  13.7 4.2 %all-to-all-start = ((bf16[2,4,768]{2,0,1:T(2,128)(2,1)}), bf16[2,4,768]{2,0,1:T(2,128)(2,1)S(1)}, u32[]{:S(2)}, u32[]{:S(2)}) async-start(bf16[2,4,768]{2,0,1:T(2,128)(2,1)} %bitcast.5), calls=%async_computation | async-start | bytes 24576 | tf_op jit(solution)/shard_map/all_to_all | solution.py:69
  17.9 0.0 all-reduce.3.cloned.1.call-start
  17.9 0.7 fusion.27
  18.6 0.7 bitcast_compare_fusion
  19.2 2.5 %all-to-all-done = bf16[2,4,768]{2,0,1:T(2,128)(2,1)S(1)} async-done(((bf16[2,4,768]{2,0,1:T(2,128)(2,1)}), bf16[2,4,768]{2,0,1:T(2,128)(2,1)S(1)}, u32[]{:S(2)}, u32[]{:S(2)}) %all-to-all-start) | async-done | bytes 12320 | tf_op jit(solution)/shard_map/all_to_all | solution.py:69
  21.8 31.3 %all_gather.3 = bf16[64,768]{1,0:T(8,128)(2,1)S(1)} all-gather(bf16[8,768]{1,0:T(8,128)(2,1)S(1)} %all_to_all.27), channel_id=1, replica_groups=mesh['attn'=4,'expert'=4,'loop'=2] {'expert','loop'}, dimensions={0}, use_global_device_ids=true | all-gather | bytes 110592 | tf_op jit(solution)/shard_map/all_gather | solution.py:70
  53.1 0.0 slice-start
  53.1 0.9 gather_fusion
  53.9 0.0 slice-start.1
  54.0 5.3 %fusion.2 = f32[128,4096]{1,0:T(8,128)} fusion(bf16[1,768,4096]{2,1,0:T(8,128)(2,1)} %param.22, bf16[128,768]{1,0:T(8,128)(2,1)S(1)} %gather_fusion, pred[128]{0:T(512)(128)(4,1)S(1)} %get-tuple-element.12, pred[128]{0:T(512)(128)(4,1)S(1)} %get-tuple-element.11), kind=kOutput, calls=%fused_computation.4 | convolution fusion | flops 805502976 | bytes 8585472 | tf_op jit(solution)/shard_map/dot_general | solution.py:78
  59.3 0.0 slice-done
  59.3 0.0 slice-done.1
  59.3 2.4 %fusion.4 = f32[128,4096]{1,0:T(8,128)} fusion(bf16[1,768,4096]{2,1,0:T(8,128)(2,1)S(1)} %bitcast.56, bf16[128,768]{1,0:T(8,128)(2,1)S(1)} %gather_fusion, pred[128]{0:T(512)(128)(4,1)S(1)} %get-tuple-element.12, pred[128]{0:T(512)(128)(4,1)S(1)} %get-tuple-element.11), kind=kOutput, calls=%fused_computation.6 | convolution fusion | flops 805502976 | bytes 8585472 | tf_op jit(solution)/shard_map/dot_general | solution.py:77
  61.7 0.0 copy-start.1
  61.7 0.0 copy-start.2
  61.7 0.0 all-reduce.3.cloned.1.call-update
  61.7 0.0 reduce-scatter.2.cloned.1.call-start
  61.7 0.6 copy-done.1
  62.3 0.0 copy-done.2
  62.3 85.1 %all-reduce.3.cloned.1.call-done = (f32[128,4096]{1,0:T(8,128)}, f32[128,4096]{1,0:T(8,128)}) async-done(((f32[128,4096]{1,0:T(8,128)}, f32[128,4096]{1,0:T(8,128)}), (f32[128,4096]{1,0:T(8,128)}, f32[128,4096]{1,0:T(8,128)})) %all-reduce.3.cloned.1.call-update) | async-done | bytes 4194320 | tf_op jit(solution)/shard_map/psum | solution.py:79
  147.5 5.3 %fusion.6 = f32[128,768]{1,0:T(8,128)S(1)} fusion(bf16[1,4096,768]{2,1,0:T(8,128)(2,1)} %param.23, f32[128,4096]{1,0:T(8,128)} %get-tuple-element.5, f32[128,4096]{1,0:T(8,128)} %get-tuple-element.6, f32[128]{0:T(128)S(1)} %bitcast_select_fusion), kind=kOutput, calls=%fused_computation.9 | convolution fusion | flops 808550400 | bytes 10879488 | tf_op jit(solution)/shard_map/dot_general | solution.py:81
  152.8 2.0 scatter_custom_fusion
  154.8 0.0 reduce-scatter.2.cloned.1.call-update
  154.9 61.3 %reduce-scatter.2.cloned.1.call-done = f32[8,768]{1,0:T(8,128)} async-done(((f32[64,768]{1,0:T(8,128)}), f32[8,768]{1,0:T(8,128)}) %reduce-scatter.2.cloned.1.call-update) | async-done | bytes 24592 | tf_op jit(solution)/shard_map/reduce_scatter | solution.py:89
  216.2 0.7 convert_element_type.45
  217.0 6.4 %all_to_all.32 = bf16[4,2,768]{2,1,0:T(2,128)(2,1)S(1)} all-to-all(bf16[4,2,768]{2,1,0:T(2,128)(2,1)S(1)} %all_to_all.28), channel_id=1, replica_groups=mesh['attn'=4,'expert'=4,'loop'=2] {'attn'}, dimensions={0} | all-to-all | bytes 24576 | tf_op jit(solution)/shard_map/all_to_all | solution.py:92
  223.3 0.6 fusion.23
  (10 shorter events, 0.1 us)
Async XLA Ops:
  6.5 2.3 %copy-start = (bf16[2,256,512]{2,1,0:T(8,128)(2,1)S(1)}, bf16[2,256,512]{2,1,0:T(8,128)(2,1)}, u32[]{:S(2)}) copy-start(bf16[2,256,512]{2,1,0:T(8,128)(2,1)} %param.15) | copy-start | bytes 1572868
  13.7 8.1 %all-to-all-start = ((bf16[2,4,768]{2,0,1:T(2,128)(2,1)}), bf16[2,4,768]{2,0,1:T(2,128)(2,1)S(1)}, u32[]{:S(2)}, u32[]{:S(2)}) async-start(bf16[2,4,768]{2,0,1:T(2,128)(2,1)} %bitcast.5), calls=%async_computation | async-start | bytes 24576 | tf_op jit(solution)/shard_map/all_to_all | solution.py:69
  17.9 129.6 %all-reduce.3.cloned.1.call-start = ((), (), s32[]{:S(2)}) async-start(), calls=%async_computation.4 | async-start | bytes 8388608 | tf_op jit(solution)/shard_map/psum | solution.py:79
  53.1 6.2 %slice-start = ((s8[6291456]{0:T(1024)(128)(4,1)}), s8[2097152]{0:T(1024)(128)(4,1)S(1)}, s32[]{:S(2)}) async-start(s8[6291456]{0:T(1024)(128)(4,1)} %bitcast.55), calls=%async_computation.5 | async-start | bytes 4194304
  53.9 5.3 %slice-start.1 = ((s8[6291456]{0:T(1024)(128)(4,1)}), s8[4194304]{0:T(1024)(128)(4,1)S(1)}, s32[]{:S(2)}) async-start(s8[6291456]{0:T(1024)(128)(4,1)} %bitcast.55), calls=%async_computation.6 | async-start | bytes 8388608
  61.7 0.7 copy-start.1
  61.7 0.7 copy-start.2
  61.7 154.5 %reduce-scatter.2.cloned.1.call-start = ((), (), s32[]{:S(2)}) async-start(), calls=%async_computation.3 | async-start | bytes 221184 | tf_op jit(solution)/shard_map/reduce_scatter | solution.py:89
Sparse Core Ops, SparseCore 0:
  61.8 85.6 all-reduce.2
  155.0 61.1 reduce-scatter.1
where the time goes:
time: 231 us
  waiting for transfers between devices  149 us (65%)
  blocking collectives  37.7 us (16%)
  matrix products  14.7 us (6%)
  between operations  13.5 us (6%)
  other arithmetic  7.93 us (3%)
  starting transfers between devices  4.28 us (2%)
  local copies, waits for them, and re-layouts  3.7 us (2%)
    psum x1, waiting for transfers between devices, per_device(): gate_total, up_total = lax.psum((gate_part, up_part), 'attn')  85.1 us
    reduce_scatter x1, waiting for transfers between devices, per_device(): lax.psum_scatter(dense_rows, ('expert', 'loop'), scatter_dimension=0, til...  61.3 us
    all_gather x1, blocking collectives, per_device(): lax.all_gather(width_parts, ('expert', 'loop'), axis=0, tiled=True)  31.3 us
    all_to_all x1, blocking collectives, per_device(): lax.all_to_all(owned_sums, 'attn', split_axis=0, concat_axis=1, tiled=True)  6.36 us
    dot_general x1, matrix products, per_device(): jnp.dot(hidden, down_weight[0], preferred_element_type=jnp.float32)  5.31 us
    dot_general x1, matrix products, per_device(): up_part = jnp.dot(picked, up_weight[0], preferred_element_type=jnp.float32)  5.31 us
  transfers between devices with their start and end apart: 3, of which 3 were waited for; matrix products, arithmetic and copies ran while one was open for 1% of the time, Pallas kernels for 0%

commit v1 on v0

--- a/solution.py
+++ b/solution.py
@@ -7,6 +7,19 @@
 KV_HEADS = 4
 HEAD = 128
 CACHE = 256
+
+
+def collect(x, axis, dim):
+    ways = lax.axis_size(axis)
+    up = [(d, (d + 1) % ways) for d in range(ways)]
+    down = [(d, (d - 1) % ways) for d in range(ways)]
+    earlier, later = ([x], [x])
+    for _ in range(ways // 2):
+        earlier.append(lax.ppermute(earlier[-1], axis, up))
+    for _ in range((ways - 1) // 2):
+        later.append(lax.ppermute(later[-1], axis, down))
+    line = jnp.concatenate([*earlier[::-1], *later[1:]], axis=dim)
+    return jnp.roll(line, (lax.axis_index(axis) - ways // 2) * x.shape[dim], axis=dim)
 
 
 def attend(query, key_cache, value_cache, new_key, new_value, cache_len):
@@ -67,7 +80,7 @@
         * norm_gain
     ).astype(jnp.bfloat16)
     width_parts = lax.all_to_all(normed, "attn", split_axis=1, concat_axis=0, tiled=True)
-    every_row = lax.all_gather(width_parts, ("expert", "loop"), axis=0, tiled=True)
+    every_row = collect(width_parts, ("expert", "loop"), 0)
     total_rows = every_row.shape[0]
     slot_total = block_rows.shape[1] * block_rows.shape[2]
     slot_rows = block_rows.reshape(slot_total)

time: 231 us -> 226 us (0.978)
  blocking collectives: 37.7 us -> 14.3 us
  starting transfers between devices: 4.28 us -> 16.1 us
  waiting for transfers between devices: 149 us -> 156 us
    all_gather x1 -> x0, blocking collectives: 31.3 us -> none  [per_device(): lax.all_gather(width_parts, ('expert', 'loop'), axis=0, tiled=True)]
    ppermute x0 -> x7, starting transfers between devices: none -> 16 us  [the longest x3 14.5 us: collect(): later.append(lax.ppermute(later[-1], axis, down))]
    ppermute x0 -> x7, waiting for transfers between devices: none -> 8.63 us  [the longest x4 7.81 us: collect(): earlier.append(lax.ppermute(earlier[-1], axis, up))]
    all_to_all x0 -> x1, blocking collectives: none -> 7.87 us  [per_device(): lax.all_to_all(normed, 'attn', split_axis=1, concat_axis=0, tiled=True)]
    all_to_all x1 -> x0, starting transfers between devices: 4.24 us -> none  [per_device(): lax.all_to_all(normed, 'attn', split_axis=1, concat_axis=0, tiled=True)]
    all_to_all x1 -> x0, waiting for transfers between devices: 2.51 us -> none  [per_device(): lax.all_to_all(normed, 'attn', split_axis=1, concat_axis=0, tiled=True)]
  transfers between devices with their start and end apart: 3 -> 9, of which waited for: 3 -> 8; matrix products, arithmetic and copies ran while one was open for 1% -> 1% of each run, Pallas kernels for 0% -> 0%
where the time goes in v1:
time: 226 us
  waiting for transfers between devices  156 us (69%)
  starting transfers between devices  16.1 us (7%)
  matrix products  14.7 us (7%)
  blocking collectives  14.3 us (6%)
  between operations  13.6 us (6%)
  other arithmetic  7.33 us (3%)
  local copies, waits for them, and re-layouts  3.77 us (2%)
    psum x1, waiting for transfers between devices, per_device(): gate_total, up_total = lax.psum((gate_part, up_part), 'attn')  85.9 us
    reduce_scatter x1, waiting for transfers between devices, per_device(): lax.psum_scatter(dense_rows, ('expert', 'loop'), scatter_dimension=0, til...  61.3 us
    ppermute x3, starting transfers between devices, collect(): later.append(lax.ppermute(later[-1], axis, down))  14.5 us
    all_to_all x1, blocking collectives, per_device(): lax.all_to_all(normed, 'attn', split_axis=1, concat_axis=0, tiled=True)  7.87 us
    ppermute x4, waiting for transfers between devices, collect(): earlier.append(lax.ppermute(earlier[-1], axis, up))  7.81 us
    all_to_all x1, blocking collectives, per_device(): lax.all_to_all(owned_sums, 'attn', split_axis=0, concat_axis=1, tiled=True)  6.38 us
    dot_general x1, matrix products, per_device(): jnp.dot(hidden, down_weight[0], preferred_element_type=jnp.float32)  5.31 us
    dot_general x1, matrix products, per_device(): up_part = jnp.dot(picked, up_weight[0], preferred_element_type=jnp.float32)  5.3 us
  transfers between devices with their start and end apart: 9, of which 8 were waited for; matrix products, arithmetic and copies ran while one was open for 1% of the time, Pallas kernels for 0%

profile of v1, /device:TPU:0, one launch (start us, length us, event | category | flops | bytes accessed | tf_op | source)
XLA Modules:
  0.0 225.7 jit_solution(12321525075945394834)
XLA Ops:
  6.5 0.0 copy-start
  6.5 0.0 all-reduce.3.cloned.1.call-start
  6.5 0.8 reshape.133
  7.3 0.7 iota_compare_fusion
  8.1 0.7 reshape.163
  8.7 0.1 fusion.30
  8.9 0.0 copy-done
  8.9 0.3 fusion.29
  9.2 0.2 fusion.17
  9.4 0.7 reshape.142
  10.1 1.3 convolution_add_fusion
  11.4 0.8 fusion.20
  12.3 0.8 fusion.22
  13.1 7.9 %all_to_all.32 = bf16[2,4,768]{2,0,1:T(2,128)(2,1)S(1)} all-to-all(bf16[2,4,768]{2,0,1:T(2,128)(2,1)S(1)} %bitcast.59), channel_id=1, replica_groups=mesh['attn'=4,'expert'=4,'loop'=2] {'attn'}, dimensions={1} | all-to-all | bytes 24576 | tf_op jit(solution)/shard_map/all_to_all | solution.py:82
  21.0 1.5 collective-permute-start
  22.5 4.9 %collective-permute-done = bf16[8,768]{1,0:T(8,128)(2,1)S(1)} collective-permute-done((bf16[8,768]{1,0:T(8,128)(2,1)S(1)}, bf16[8,768]{1,0:T(8,128)(2,1)S(1)}, u32[]{:S(2)}, u32[]{:S(2)}) %collective-permute-start) | collective-permute-done | bytes 12320 | tf_op jit(solution)/shard_map/ppermute | solution.py:18
  27.4 0.0 collective-permute-start.1
  27.4 0.7 fusion.27
  28.1 4.7 %collective-permute-start.4 = (bf16[8,768]{1,0:T(8,128)(2,1)S(1)}, bf16[8,768]{1,0:T(8,128)(2,1)S(1)}, u32[]{:S(2)}, u32[]{:S(2)}) collective-permute-start(bf16[8,768]{1,0:T(8,128)(2,1)S(1)} %all_to_all.27), channel_id=1, source_target_pairs={{0,7},{1,0},{2,1},{3,2},{4,3},{5,4},{6,5},{7,6},{8,15},{9,8},{10,9... | collective-permute-start | bytes 36872 | tf_op jit(solution)/shard_map/ppermute | solution.py:20
  32.8 1.0 collective-permute-done.1
  33.8 0.0 collective-permute-start.2
  33.8 0.7 bitcast_compare_fusion
  34.5 0.0 collective-permute-done.4
  34.5 4.8 %collective-permute-start.5 = (bf16[8,768]{1,0:T(8,128)(2,1)S(1)}, bf16[8,768]{1,0:T(8,128)(2,1)S(1)}, u32[]{:S(2)}, u32[]{:S(2)}) collective-permute-start(bf16[8,768]{1,0:T(8,128)(2,1)S(1)} %collective-permute-done.4), channel_id=1, source_target_pairs={{0,7},{1,0},{2,1},{3,2},{4,3},{5,4},{6,5},{7,6},{8,15},{9,8},{10,9... | collective-permute-start | bytes 36872 | tf_op jit(solution)/shard_map/ppermute | solution.py:20
  39.2 0.9 collective-permute-done.2
  40.2 0.0 collective-permute-start.3
  40.2 0.4 collective-permute-done.5
  40.6 5.0 %collective-permute-start.6 = (bf16[8,768]{1,0:T(8,128)(2,1)S(1)}, bf16[8,768]{1,0:T(8,128)(2,1)S(1)}, u32[]{:S(2)}, u32[]{:S(2)}) collective-permute-start(bf16[8,768]{1,0:T(8,128)(2,1)S(1)} %collective-permute-done.5), channel_id=1, source_target_pairs={{0,7},{1,0},{2,1},{3,2},{4,3},{5,4},{6,5},{7,6},{8,15},{9,8},{10,9... | collective-permute-start | bytes 36872 | tf_op jit(solution)/shard_map/ppermute | solution.py:20
  45.6 0.9 collective-permute-done.3
  46.6 0.4 collective-permute-done.6
  47.1 0.0 slice-start
  47.1 0.9 gather_fusion
  48.0 0.0 slice-start.1
  48.0 5.3 %fusion.2 = f32[128,4096]{1,0:T(8,128)} fusion(bf16[1,768,4096]{2,1,0:T(8,128)(2,1)} %param.22, bf16[128,768]{1,0:T(8,128)(2,1)S(1)} %gather_fusion, pred[128]{0:T(512)(128)(4,1)S(1)} %get-tuple-element.12, pred[128]{0:T(512)(128)(4,1)S(1)} %get-tuple-element.11), kind=kOutput, calls=%fused_computation.4 | convolution fusion | flops 805502976 | bytes 8585472 | tf_op jit(solution)/shard_map/dot_general | solution.py:91
  53.3 0.0 slice-done
  53.3 2.4 %fusion.4 = f32[128,4096]{1,0:T(8,128)} fusion(bf16[1,768,4096]{2,1,0:T(8,128)(2,1)S(1)} %bitcast.56, bf16[128,768]{1,0:T(8,128)(2,1)S(1)} %gather_fusion, pred[128]{0:T(512)(128)(4,1)S(1)} %get-tuple-element.12, pred[128]{0:T(512)(128)(4,1)S(1)} %get-tuple-element.11), kind=kOutput, calls=%fused_computation.6 | convolution fusion | flops 805502976 | bytes 8585472 | tf_op jit(solution)/shard_map/dot_general | solution.py:90
  55.7 0.0 all-reduce.3.cloned.1.call-update
  55.8 0.0 reduce-scatter.2.cloned.1.call-start
  55.8 0.6 copy-done.1
  56.4 0.0 copy-done.2
  56.4 85.9 %all-reduce.3.cloned.1.call-done = (f32[128,4096]{1,0:T(8,128)}, f32[128,4096]{1,0:T(8,128)}) async-done(((f32[128,4096]{1,0:T(8,128)}, f32[128,4096]{1,0:T(8,128)}), (f32[128,4096]{1,0:T(8,128)}, f32[128,4096]{1,0:T(8,128)})) %all-reduce.3.cloned.1.call-update) | async-done | bytes 4194320 | tf_op jit(solution)/shard_map/psum | solution.py:92
  142.4 5.3 %fusion.6 = f32[128,768]{1,0:T(8,128)S(1)} fusion(bf16[1,4096,768]{2,1,0:T(8,128)(2,1)} %param.23, f32[128,4096]{1,0:T(8,128)} %get-tuple-element.5, f32[128,4096]{1,0:T(8,128)} %get-tuple-element.6, f32[128]{0:T(128)S(1)} %bitcast_select_fusion), kind=kOutput, calls=%fused_computation.9 | convolution fusion | flops 808550400 | bytes 10879488 | tf_op jit(solution)/shard_map/dot_general | solution.py:94
  147.7 2.0 scatter_custom_fusion
  149.7 0.0 reduce-scatter.2.cloned.1.call-update
  149.7 61.3 %reduce-scatter.2.cloned.1.call-done = f32[8,768]{1,0:T(8,128)} async-done(((f32[64,768]{1,0:T(8,128)}), f32[8,768]{1,0:T(8,128)}) %reduce-scatter.2.cloned.1.call-update) | async-done | bytes 24592 | tf_op jit(solution)/shard_map/reduce_scatter | solution.py:102
  211.1 0.7 convert_element_type.45
  211.8 6.4 %all_to_all.33 = bf16[4,2,768]{2,1,0:T(2,128)(2,1)S(1)} all-to-all(bf16[4,2,768]{2,1,0:T(2,128)(2,1)S(1)} %all_to_all.28), channel_id=1, replica_groups=mesh['attn'=4,'expert'=4,'loop'=2] {'attn'}, dimensions={0} | all-to-all | bytes 24576 | tf_op jit(solution)/shard_map/all_to_all | solution.py:105
  218.2 0.6 fusion.23
  (30 shorter events, 0.2 us)
Async XLA Ops:
  6.5 2.3 %copy-start = (bf16[2,256,512]{2,1,0:T(8,128)(2,1)S(1)}, bf16[2,256,512]{2,1,0:T(8,128)(2,1)}, u32[]{:S(2)}) copy-start(bf16[2,256,512]{2,1,0:T(8,128)(2,1)} %param.15) | copy-start | bytes 1572868
  6.5 135.8 %all-reduce.3.cloned.1.call-start = ((), (), s32[]{:S(2)}) async-start(), calls=%async_computation.4 | async-start | bytes 8388608 | tf_op jit(solution)/shard_map/psum | solution.py:92
  21.0 6.4 %collective-permute-start = (bf16[8,768]{1,0:T(8,128)(2,1)S(1)}, bf16[8,768]{1,0:T(8,128)(2,1)S(1)}, u32[]{:S(2)}, u32[]{:S(2)}) collective-permute-start(bf16[8,768]{1,0:T(8,128)(2,1)S(1)} %all_to_all.27), channel_id=1, source_target_pairs={{0,1},{1,2},{2,3},{3,4},{4,5},{5,6},{6,7},{7,0},{8,9},{9,10},{10,1... | collective-permute-start | bytes 36872 | tf_op jit(solution)/shard_map/ppermute | solution.py:18
  27.4 6.4 %collective-permute-start.1 = (bf16[8,768]{1,0:T(8,128)(2,1)S(1)}, bf16[8,768]{1,0:T(8,128)(2,1)S(1)}, u32[]{:S(2)}, u32[]{:S(2)}) collective-permute-start(bf16[8,768]{1,0:T(8,128)(2,1)S(1)} %collective-permute-done), channel_id=1, source_target_pairs={{0,1},{1,2},{2,3},{3,4},{4,5},{5,6},{6,7},{7,0},{8,9},{9,10},{10,1... | collective-permute-start | bytes 36872 | tf_op jit(solution)/shard_map/ppermute | solution.py:18
  28.1 6.4 %collective-permute-start.4 = (bf16[8,768]{1,0:T(8,128)(2,1)S(1)}, bf16[8,768]{1,0:T(8,128)(2,1)S(1)}, u32[]{:S(2)}, u32[]{:S(2)}) collective-permute-start(bf16[8,768]{1,0:T(8,128)(2,1)S(1)} %all_to_all.27), channel_id=1, source_target_pairs={{0,7},{1,0},{2,1},{3,2},{4,3},{5,4},{6,5},{7,6},{8,15},{9,8},{10,9... | collective-permute-start | bytes 36872 | tf_op jit(solution)/shard_map/ppermute | solution.py:20
  33.8 6.4 %collective-permute-start.2 = (bf16[8,768]{1,0:T(8,128)(2,1)S(1)}, bf16[8,768]{1,0:T(8,128)(2,1)S(1)}, u32[]{:S(2)}, u32[]{:S(2)}) collective-permute-start(bf16[8,768]{1,0:T(8,128)(2,1)S(1)} %collective-permute-done.1), channel_id=1, source_target_pairs={{0,1},{1,2},{2,3},{3,4},{4,5},{5,6},{6,7},{7,0},{8,9},{9,10},{10,1... | collective-permute-start | bytes 36872 | tf_op jit(solution)/shard_map/ppermute | solution.py:18
  34.5 6.2 %collective-permute-start.5 = (bf16[8,768]{1,0:T(8,128)(2,1)S(1)}, bf16[8,768]{1,0:T(8,128)(2,1)S(1)}, u32[]{:S(2)}, u32[]{:S(2)}) collective-permute-start(bf16[8,768]{1,0:T(8,128)(2,1)S(1)} %collective-permute-done.4), channel_id=1, source_target_pairs={{0,7},{1,0},{2,1},{3,2},{4,3},{5,4},{6,5},{7,6},{8,15},{9,8},{10,9... | collective-permute-start | bytes 36872 | tf_op jit(solution)/shard_map/ppermute | solution.py:20
  40.2 6.4 %collective-permute-start.3 = (bf16[8,768]{1,0:T(8,128)(2,1)S(1)}, bf16[8,768]{1,0:T(8,128)(2,1)S(1)}, u32[]{:S(2)}, u32[]{:S(2)}) collective-permute-start(bf16[8,768]{1,0:T(8,128)(2,1)S(1)} %collective-permute-done.2), channel_id=1, source_target_pairs={{0,1},{1,2},{2,3},{3,4},{4,5},{5,6},{6,7},{7,0},{8,9},{9,10},{10,1... | collective-permute-start | bytes 36872 | tf_op jit(solution)/shard_map/ppermute | solution.py:18
  40.6 6.4 %collective-permute-start.6 = (bf16[8,768]{1,0:T(8,128)(2,1)S(1)}, bf16[8,768]{1,0:T(8,128)(2,1)S(1)}, u32[]{:S(2)}, u32[]{:S(2)}) collective-permute-start(bf16[8,768]{1,0:T(8,128)(2,1)S(1)} %collective-permute-done.5), channel_id=1, source_target_pairs={{0,7},{1,0},{2,1},{3,2},{4,3},{5,4},{6,5},{7,6},{8,15},{9,8},{10,9... | collective-permute-start | bytes 36872 | tf_op jit(solution)/shard_map/ppermute | solution.py:20
  47.1 6.2 %slice-start = ((s8[6291456]{0:T(1024)(128)(4,1)}), s8[2097152]{0:T(1024)(128)(4,1)S(1)}, s32[]{:S(2)}) async-start(s8[6291456]{0:T(1024)(128)(4,1)} %bitcast.55), calls=%async_computation.5 | async-start | bytes 4194304
  48.0 5.3 %slice-start.1 = ((s8[6291456]{0:T(1024)(128)(4,1)}), s8[4194304]{0:T(1024)(128)(4,1)S(1)}, s32[]{:S(2)}) async-start(s8[6291456]{0:T(1024)(128)(4,1)} %bitcast.55), calls=%async_computation.6 | async-start | bytes 8388608
  55.7 0.7 copy-start.1
  55.7 0.7 copy-start.2
  55.8 155.3 %reduce-scatter.2.cloned.1.call-start = ((), (), s32[]{:S(2)}) async-start(), calls=%async_computation.3 | async-start | bytes 221184 | tf_op jit(solution)/shard_map/reduce_scatter | solution.py:102
Sparse Core Ops, SparseCore 0:
  55.9 86.4 all-reduce.2
  149.9 61.1 reduce-scatter.1
